TPU v7x, 32 devices: a whole 2x2x4 slice. The times are simulated.
32 devices in a mesh: dp: 8 (over z, y), tp: 4 (over x, core).
Axes of the slice: x: 2, y: 2, z: 4, core: 2. Of those that a mesh axis runs over, the one named last changes fastest.
Arguments:
- frames: bfloat16 [24, 1024, 512], P('dp', 'tp'), may hold values from -6 to 6
- cotangent: bfloat16 [24, 1024, 512], P('dp', 'tp'), may hold values from -6 to 6
- lengths: int32 [24], P('dp'), may hold values from 64 to 1024, as said below
- conv_weight: float32 [512, 7], P(('dp', 'tp')), may hold values from -2 to 2
- conv_bias: float32 [512], P(('dp', 'tp')), may hold values from -0.6 to 0.6
- norm_gain: float32 [512], P(('dp', 'tp')), may hold values from 0.5 to 1.5
- norm_bias: float32 [512], P(('dp', 'tp')), may hold values from -0.6 to 0.6
- up_weight: float32 [512, 1536], P('dp', 'tp'), may hold values from -0.25 to 0.25
- up_bias: float32 [1536], P(('dp', 'tp')), may hold values from -0.6 to 0.6
- down_weight: float32 [512, 1536], P('dp', 'tp'), may hold values from -0.15625 to 0.15625
- down_bias: float32 [512], P(('dp', 'tp')), may hold values from -0.6 to 0.6
- layer_scale: float32 [512], P(('dp', 'tp')), may hold values from 0.25 to 1.75
- moment_conv_weight: float32 [512, 7], P(('dp', 'tp')), may hold values from -36 to 36
- moment_conv_bias: float32 [512], P(('dp', 'tp')), may hold values from -36 to 36
- moment_norm_gain: float32 [512], P(('dp', 'tp')), may hold values from -36 to 36
- moment_norm_bias: float32 [512], P(('dp', 'tp')), may hold values from -36 to 36
- moment_up_weight: float32 [512, 1536], P('dp', 'tp'), may hold values from -36 to 36
- moment_up_bias: float32 [1536], P(('dp', 'tp')), may hold values from -36 to 36
- moment_down_weight: float32 [512, 1536], P('dp', 'tp'), may hold values from -36 to 36
- moment_down_bias: float32 [512], P(('dp', 'tp')), may hold values from -36 to 36
- moment_layer_scale: float32 [512], P(('dp', 'tp')), may hold values from -36 to 36
- square_conv_weight: float32 [512, 7], P(('dp', 'tp')), may hold values from 1 to 9
- square_conv_bias: float32 [512], P(('dp', 'tp')), may hold values from 1 to 9
- square_norm_gain: float32 [512], P(('dp', 'tp')), may hold values from 1 to 9
- square_norm_bias: float32 [512], P(('dp', 'tp')), may hold values from 1 to 9
- square_up_weight: float32 [512, 1536], P('dp', 'tp'), may hold values from 1 to 9
- square_up_bias: float32 [1536], P(('dp', 'tp')), may hold values from 1 to 9
- square_down_weight: float32 [512, 1536], P('dp', 'tp'), may hold values from 1 to 9
- square_down_bias: float32 [512], P(('dp', 'tp')), may hold values from 1 to 9
- square_layer_scale: float32 [512], P(('dp', 'tp')), may hold values from 1 to 9
Outputs:
- output: float32 [24, 1024, 512], P('dp', 'tp')
- input_grad: float32 [24, 1024, 512], P('dp', 'tp')
- grad_conv_weight: float32 [512, 7], P(('dp', 'tp'))
- next_conv_weight: float32 [512, 7], P(('dp', 'tp'))
- next_moment_conv_weight: float32 [512, 7], P(('dp', 'tp'))
- next_square_conv_weight: float32 [512, 7], P(('dp', 'tp'))
- grad_conv_bias: float32 [512], P(('dp', 'tp'))
- next_conv_bias: float32 [512], P(('dp', 'tp'))
- next_moment_conv_bias: float32 [512], P(('dp', 'tp'))
- next_square_conv_bias: float32 [512], P(('dp', 'tp'))
- grad_norm_gain: float32 [512], P(('dp', 'tp'))
- update_norm_gain: float32 [512], P(('dp', 'tp'))
- next_moment_norm_gain: float32 [512], P(('dp', 'tp'))
- next_square_norm_gain: float32 [512], P(('dp', 'tp'))
- grad_norm_bias: float32 [512], P(('dp', 'tp'))
- next_norm_bias: float32 [512], P(('dp', 'tp'))
- next_moment_norm_bias: float32 [512], P(('dp', 'tp'))
- next_square_norm_bias: float32 [512], P(('dp', 'tp'))
- grad_up_weight: float32 [512, 1536], P('dp', 'tp')
- next_up_weight: float32 [512, 1536], P('dp', 'tp')
- next_moment_up_weight: float32 [512, 1536], P('dp', 'tp')
- next_square_up_weight: float32 [512, 1536], P('dp', 'tp')
- grad_up_bias: float32 [1536], P(('dp', 'tp'))
- next_up_bias: float32 [1536], P(('dp', 'tp'))
- next_moment_up_bias: float32 [1536], P(('dp', 'tp'))
- next_square_up_bias: float32 [1536], P(('dp', 'tp'))
- grad_down_weight: float32 [512, 1536], P('dp', 'tp')
- next_down_weight: float32 [512, 1536], P('dp', 'tp')
- next_moment_down_weight: float32 [512, 1536], P('dp', 'tp')
- next_square_down_weight: float32 [512, 1536], P('dp', 'tp')
- grad_down_bias: float32 [512], P(('dp', 'tp'))
- next_down_bias: float32 [512], P(('dp', 'tp'))
- next_moment_down_bias: float32 [512], P(('dp', 'tp'))
- next_square_down_bias: float32 [512], P(('dp', 'tp'))
- grad_layer_scale: float32 [512], P(('dp', 'tp'))
- update_layer_scale: float32 [512], P(('dp', 'tp'))
- next_moment_layer_scale: float32 [512], P(('dp', 'tp'))
- next_square_layer_scale: float32 [512], P(('dp', 'tp'))
Inputs may be any that keep to these rules, and one draw needn't show every extreme that they name: `lengths`: each slot's true frame count lies between 64 and 1024; in every draw at least one slot holds 1024 true frames.
All inputs are finite; a program needn't handle non-finite values.
Results may differ from a plain program's by a relative error of at most 0.0079.
Values may be sent and summed in bfloat16 or wider, within the bound.
No kernel may reach another device: no remote copies, remote signals or barrier semaphores. Data moves between devices by JAX's collectives and lax.ppermute only.
A program may use at most 128 MiB of HBM per device.

v0:
```python
import jax
import jax.numpy as jnp
from jax import lax
from jax.sharding import PartitionSpec as P

STEP = 4
norm_eps = 1e-06
learn_rate = 0.05
first_decay = 0.9
second_decay = 0.999
adam_eps = 1e-08
weight_decay = 0.1
update_flags = (False, False, True, False, False, False, False, False, True)


def conv_apply(padded, tap_weights, conv_shift, frames_out):
    result = conv_shift + padded[:, 0:frames_out, :] * tap_weights[:, 0]
    for offset in range(1, tap_weights.shape[1]):
        result = result + padded[:, offset : offset + frames_out, :] * tap_weights[:, offset]
    return result


def conv_back(grad_padded, tap_weights, frames_out):
    edge_start = tap_weights.shape[1] - 1
    result = grad_padded[:, edge_start : edge_start + frames_out, :] * tap_weights[:, 0]
    for offset in range(1, tap_weights.shape[1]):
        begin = edge_start - offset
        result = result + grad_padded[:, begin : begin + frames_out, :] * tap_weights[:, offset]
    return result


def tap_grads(conv_grad, padded):
    frames_out = conv_grad.shape[1]
    tap_total = padded.shape[1] - frames_out + 1
    columns = [
        jnp.sum(conv_grad * padded[:, offset : offset + frames_out, :], axis=(0, 1))
        for offset in range(tap_total)
    ]
    return jnp.stack(columns, axis=1)


def norm_forward(conv_out, gain_vector, shift_vector):
    centred = conv_out - jnp.mean(conv_out, axis=-1, keepdims=True)
    inverse = lax.rsqrt(jnp.mean(centred * centred, axis=-1, keepdims=True) + norm_eps)
    unit_norm = centred * inverse
    return (unit_norm * gain_vector + shift_vector, unit_norm, inverse)


def norm_backward(normed_grad, unit_norm, inverse, gain_vector):
    scaled = normed_grad * gain_vector
    centred_grad = scaled - jnp.mean(scaled, axis=-1, keepdims=True)
    return inverse * (
        centred_grad - unit_norm * jnp.mean(scaled * unit_norm, axis=-1, keepdims=True)
    )


def exact_gelu(values):
    return jax.nn.gelu(values, approximate=False)


def adam_step(weights_now, gradient, moment, square, step_number):
    next_moment = first_decay * moment + (1.0 - first_decay) * gradient
    next_square = second_decay * square + (1.0 - second_decay) * gradient * gradient
    first_fix = 1.0 - jnp.power(jnp.float32(first_decay), step_number)
    second_fix = 1.0 - jnp.power(jnp.float32(second_decay), step_number)
    step_ratio = next_moment / first_fix / (jnp.sqrt(next_square / second_fix) + adam_eps)
    update = -(learn_rate * (step_ratio + weight_decay * weights_now))
    return (weights_now + update, next_moment, next_square, update)


def per_device(
    frames,
    cotangent,
    lengths,
    conv_weight,
    conv_bias,
    norm_gain,
    norm_bias,
    up_weight,
    up_bias,
    down_weight,
    down_bias,
    layer_scale,
    moment_conv_weight,
    moment_conv_bias,
    moment_norm_gain,
    moment_norm_bias,
    moment_up_weight,
    moment_up_bias,
    moment_down_weight,
    moment_down_bias,
    moment_layer_scale,
    square_conv_weight,
    square_conv_bias,
    square_norm_gain,
    square_norm_bias,
    square_up_weight,
    square_up_bias,
    square_down_weight,
    square_down_bias,
    square_layer_scale,
):
    tp_count = lax.axis_size("tp")
    device_rank = lax.axis_index("tp")
    slot_count, quarter_len, feature_width = frames.shape
    slot_len = quarter_len * tp_count
    frame_start = device_rank * quarter_len
    up_rows, down_rows = (
        lax.all_gather(up_weight.astype(jnp.bfloat16), "dp", axis=0, tiled=True),
        lax.all_gather(down_weight.astype(jnp.bfloat16), "dp", axis=0, tiled=True),
    )
    tap_weights, conv_shift, gain_vector, shift_vector, up_shift, down_shift, scale_vector = (
        lax.all_gather(conv_weight, ("dp", "tp"), axis=0, tiled=True),
        lax.all_gather(conv_bias, ("dp", "tp"), axis=0, tiled=True),
        lax.all_gather(norm_gain, ("dp", "tp"), axis=0, tiled=True),
        lax.all_gather(norm_bias, ("dp", "tp"), axis=0, tiled=True),
        lax.all_gather(up_bias, ("dp", "tp"), axis=0, tiled=True),
        lax.all_gather(down_bias, ("dp", "tp"), axis=0, tiled=True),
        lax.all_gather(layer_scale, ("dp", "tp"), axis=0, tiled=True),
    )
    kernel_half = tap_weights.shape[1] // 2
    hidden_width = up_shift.shape[0]
    own_width = up_rows.shape[1]
    whole_frames, whole_cot = (
        lax.all_gather(frames, "tp", axis=1, tiled=True),
        lax.all_gather(cotangent, "tp", axis=1, tiled=True),
    )
    positions = lax.broadcasted_iota(jnp.int32, (slot_count, slot_len), 1)
    frame_mask = (positions < lengths[:, None]).astype(jnp.float32)[:, :, None]
    signal = whole_frames.astype(jnp.float32)
    shifted = signal * frame_mask
    padded = jnp.pad(shifted, ((0, 0), (kernel_half, kernel_half), (0, 0)))
    conv_out = conv_apply(padded, tap_weights, conv_shift, slot_len)
    normed, unit_norm, inverse = norm_forward(conv_out, gain_vector, shift_vector)
    normed_low = normed.astype(jnp.bfloat16)
    own_shift = lax.dynamic_slice_in_dim(up_shift, device_rank * own_width, own_width)
    hidden = (
        jnp.einsum("slc,ch->slh", normed_low, up_rows, preferred_element_type=jnp.float32)
        + own_shift
    )
    active, gelu_pull = jax.vjp(exact_gelu, hidden)
    active_low = active.astype(jnp.bfloat16)
    partial_out = jnp.einsum(
        "slh,ch->slc", active_low, down_rows, preferred_element_type=jnp.float32
    )
    branch = lax.psum(partial_out, "tp") + down_shift
    output_full = (signal + scale_vector * branch) * frame_mask
    back_grad = whole_cot.astype(jnp.float32) * frame_mask
    branch_grad = (back_grad * scale_vector).astype(jnp.bfloat16)
    active_grad = jnp.einsum(
        "slc,ch->slh", branch_grad, down_rows, preferred_element_type=jnp.float32
    )
    hidden_grad = gelu_pull(active_grad)[0].astype(jnp.bfloat16)
    normed_part = jnp.einsum(
        "slh,ch->slc", hidden_grad, up_rows, preferred_element_type=jnp.float32
    )
    normed_grad = lax.psum(normed_part, "tp")
    conv_grad = norm_backward(normed_grad, unit_norm, inverse, gain_vector)
    grad_padded = jnp.pad(conv_grad, ((0, 0), (kernel_half, kernel_half), (0, 0)))
    input_full = back_grad + frame_mask * conv_back(grad_padded, tap_weights, slot_len)
    grad_up = jnp.einsum("slc,slh->ch", normed_low, hidden_grad, preferred_element_type=jnp.float32)
    grad_down = jnp.einsum(
        "slc,slh->ch", branch_grad, active_low, preferred_element_type=jnp.float32
    )
    own_up_grad = jnp.sum(hidden_grad.astype(jnp.float32), axis=(0, 1))
    grad_up_shift = lax.dynamic_update_slice_in_dim(
        jnp.zeros((hidden_width,), jnp.float32), own_up_grad, device_rank * own_width, 0
    )

    def own_frames(values):
        return lax.dynamic_slice_in_dim(values, frame_start, quarter_len, 1)

    conv_grad_own = own_frames(conv_grad)
    normed_grad_own = own_frames(normed_grad)
    unit_own = own_frames(unit_norm)
    back_own = own_frames(back_grad)
    branch_own = own_frames(branch)
    branch_grad_own = own_frames(branch_grad)
    taps_grad = tap_grads(
        conv_grad_own,
        lax.dynamic_slice_in_dim(padded, frame_start, quarter_len + 2 * kernel_half, 1),
    )
    output_own = own_frames(output_full)
    input_own = own_frames(input_full)
    grad_scale = jnp.sum(back_own * branch_own, axis=(0, 1))
    grad_down_shift = jnp.sum(branch_grad_own.astype(jnp.float32), axis=(0, 1))
    grad_gain = jnp.sum(normed_grad_own * unit_own, axis=(0, 1))
    grad_shift = jnp.sum(normed_grad_own, axis=(0, 1))
    grad_conv_shift = jnp.sum(conv_grad_own, axis=(0, 1))
    up_share, down_share = (
        lax.psum_scatter(grad_up, "dp", scatter_dimension=0, tiled=True),
        lax.psum_scatter(grad_down, "dp", scatter_dimension=0, tiled=True),
    )
    share_taps, share_conv, share_gain, share_shift, share_up, share_down, share_scale = (
        lax.psum_scatter(taps_grad, ("dp", "tp"), scatter_dimension=0, tiled=True),
        lax.psum_scatter(grad_conv_shift, ("dp", "tp"), scatter_dimension=0, tiled=True),
        lax.psum_scatter(grad_gain, ("dp", "tp"), scatter_dimension=0, tiled=True),
        lax.psum_scatter(grad_shift, ("dp", "tp"), scatter_dimension=0, tiled=True),
        lax.psum_scatter(grad_up_shift, ("dp", "tp"), scatter_dimension=0, tiled=True),
        lax.psum_scatter(grad_down_shift, ("dp", "tp"), scatter_dimension=0, tiled=True),
        lax.psum_scatter(grad_scale, ("dp", "tp"), scatter_dimension=0, tiled=True),
    )
    step_number = jnp.float32(STEP)
    params = (
        conv_weight,
        conv_bias,
        norm_gain,
        norm_bias,
        up_weight,
        up_bias,
        down_weight,
        down_bias,
        layer_scale,
    )
    gradients = (
        share_taps,
        share_conv,
        share_gain,
        share_shift,
        up_share,
        share_up,
        down_share,
        share_down,
        share_scale,
    )
    moments = (
        moment_conv_weight,
        moment_conv_bias,
        moment_norm_gain,
        moment_norm_bias,
        moment_up_weight,
        moment_up_bias,
        moment_down_weight,
        moment_down_bias,
        moment_layer_scale,
    )
    squares = (
        square_conv_weight,
        square_conv_bias,
        square_norm_gain,
        square_norm_bias,
        square_up_weight,
        square_up_bias,
        square_down_weight,
        square_down_bias,
        square_layer_scale,
    )
    flat = [output_own, input_own]
    for weights_now, gradient, moment, square, use_update in zip(
        params, gradients, moments, squares, update_flags
    ):
        next_weights, next_moment, next_square, update = adam_step(
            weights_now, gradient, moment, square, step_number
        )
        shown = update if use_update else next_weights
        flat = flat + [gradient, shown, next_moment, next_square]
    return (
        flat[0],
        flat[1],
        flat[2],
        flat[3],
        flat[4],
        flat[5],
        flat[6],
        flat[7],
        flat[8],
        flat[9],
        flat[10],
        flat[11],
        flat[12],
        flat[13],
        flat[14],
        flat[15],
        flat[16],
        flat[17],
        flat[18],
        flat[19],
        flat[20],
        flat[21],
        flat[22],
        flat[23],
        flat[24],
        flat[25],
        flat[26],
        flat[27],
        flat[28],
        flat[29],
        flat[30],
        flat[31],
        flat[32],
        flat[33],
        flat[34],
        flat[35],
        flat[36],
        flat[37],
    )


def solution(mesh):
    return jax.shard_map(
        per_device,
        mesh=mesh,
        in_specs=(
            P("dp", "tp", None),
            P("dp", "tp", None),
            P("dp"),
            P(("dp", "tp"), None),
            P(("dp", "tp")),
            P(("dp", "tp")),
            P(("dp", "tp")),
            P("dp", "tp"),
            P(("dp", "tp")),
            P("dp", "tp"),
            P(("dp", "tp")),
            P(("dp", "tp")),
            P(("dp", "tp"), None),
            P(("dp", "tp")),
            P(("dp", "tp")),
            P(("dp", "tp")),
            P("dp", "tp"),
            P(("dp", "tp")),
            P("dp", "tp"),
            P(("dp", "tp")),
            P(("dp", "tp")),
            P(("dp", "tp"), None),
            P(("dp", "tp")),
            P(("dp", "tp")),
            P(("dp", "tp")),
            P("dp", "tp"),
            P(("dp", "tp")),
            P("dp", "tp"),
            P(("dp", "tp")),
            P(("dp", "tp")),
        ),
        out_specs=(
            P("dp", "tp", None),
            P("dp", "tp", None),
            P(("dp", "tp"), None),
            P(("dp", "tp"), None),
            P(("dp", "tp"), None),
            P(("dp", "tp"), None),
            P(("dp", "tp")),
            P(("dp", "tp")),
            P(("dp", "tp")),
            P(("dp", "tp")),
            P(("dp", "tp")),
            P(("dp", "tp")),
            P(("dp", "tp")),
            P(("dp", "tp")),
            P(("dp", "tp")),
            P(("dp", "tp")),
            P(("dp", "tp")),
            P(("dp", "tp")),
            P("dp", "tp"),
            P("dp", "tp"),
            P("dp", "tp"),
            P("dp", "tp"),
            P(("dp", "tp")),
            P(("dp", "tp")),
            P(("dp", "tp")),
            P(("dp", "tp")),
            P("dp", "tp"),
            P("dp", "tp"),
            P("dp", "tp"),
            P("dp", "tp"),
            P(("dp", "tp")),
            P(("dp", "tp")),
            P(("dp", "tp")),
            P(("dp", "tp")),
            P(("dp", "tp")),
            P(("dp", "tp")),
            P(("dp", "tp")),
            P(("dp", "tp")),
        ),
        check_vma=False,
    )
```

profile of v0, /device:TPU:0, one launch (start us, length us, event | category | flops | bytes accessed | tf_op | source)
XLA Modules:
  0.0 722.1 jit_solution(14380153058658341902)
XLA Ops:
  9.7 44.2 %all-gather = f32[32,16,7]{1,2,0:T(8,128)S(1)} all-gather(f32[1,16,7]{1,2,0:T(8,128)} %bitcast.62), channel_id=1, replica_groups=mesh['dp'=8,'tp'=4] {'dp','tp'}, dimensions={0}, use_global_device_ids=true | all-gather | bytes 14784 | tf_op jit(solution)/shard_map/all_gather | solution.py:113
  59.1 37.4 %all-reduce.15 = (f32[512]{0:T(512)S(1)}, f32[512]{0:T(512)S(1)}, f32[512]{0:T(512)S(1)}, f32[1536]{0:T(1024)S(1)}, f32[512]{0:T(512)S(1)}, /*index=5*/f32[512]{0:T(512)S(1)}) all-reduce(f32[512]{0:T(512)S(1)} %dynamic-update-slice.1, f32[512]{0:T(512)S(1)} %dynamic-update-slice.3, ...), channel_id=1, replica_groups=mesh['dp'=8,'tp'=4] {'dp','tp'}, use_global_device_ids=true, to_apply=%add.3 | all-reduce | flops 4096 | bytes 32768
  96.5 31.3 %all_gather.39 = bf16[512,384]{1,0:T(8,128)(2,1)S(1)} all-gather(bf16[64,384]{1,0:T(8,128)(2,1)S(1)} %convert_element_type.43), channel_id=1, replica_groups=mesh['dp'=8,'tp'=4] {'dp'}, dimensions={0}, use_global_device_ids=true | all-gather | bytes 442368 | tf_op jit(solution)/shard_map/all_gather | solution.py:109
  128.6 5.2 convert_multiply_fusion
  133.8 6.0 fusion.59
  142.4 3.1 fusion.31
  145.6 11.7 %multiply_convert_fusion.1 = (bf16[3,1024,384]{2,1,0:T(8,128)(2,1)S(1)}, f32[3,1024,384]{2,1,0:T(8,128)}) fusion(f32[3,1024,384]{2,1,0:T(8,128)S(1)} %get-tuple-element.123, f32[384]{0:T(512)S(1)} %dynamic_slice.30, u8[1024,384]{1,0:T(8,128)(4,1)S(1)} %get-tuple-element.51, u8[1024,384]{1,0:T(8,128)(4,1)S(1)} %get-tuple-element.50), kind=kLoop, calls=%fused_computation.35 | loop fusion | flops 83755008 | bytes 12584448 | tf_op jit(solution)/shard_map/convert_element_type | solution.py:142
  157.4 2.7 convolution_bitcast_fusion
  160.3 63.0 %reduce-scatter.8.cloned.1.call-done = f32[64,384]{1,0:T(8,128)} async-done(((f32[512,384]{1,0:T(8,128)}), f32[64,384]{1,0:T(8,128)}) %reduce-scatter.8.cloned.1.call-update) | async-done | bytes 98320 | tf_op jit(solution)/shard_map/reduce_scatter | solution.py:192
  225.1 31.1 %all_gather.41 = bf16[512,384]{1,0:T(8,128)(2,1)S(1)} all-gather(bf16[64,384]{1,0:T(8,128)(2,1)S(1)} %get-tuple-element.114), channel_id=1, replica_groups=mesh['dp'=8,'tp'=4] {'dp'}, dimensions={0}, use_global_device_ids=true | all-gather | bytes 442368 | tf_op jit(solution)/shard_map/all_gather | solution.py:110
  256.2 8.1 %convert_reduce_fusion = (f32[384]{0:T(512)S(1)}, bf16[3,1024,384]{2,1,0:T(8,128)(2,1)S(1)}) fusion(f32[3,1024,384]{2,1,0:T(8,128)} %get-tuple-element.102, bf16[3,1024,512]{2,1,0:T(8,128)(2,1)} %copy-done.4, bf16[512,384]{1,0:T(8,128)(2,1)S(1)} %all_gather.41, f32[3,1024,384]{2,1,0:T(8,128)} %copy-done.7, f32[384]{0:T(512)S(1)} %dynamic_slice.30), kind=kOutput, calls=%fused_computation.33 | convolution fusion | flops 1228013184 | bytes 15338496 | tf_op jit(solution)/shard_map/slc,ch->slh/dot_general | solution.py:150
  265.7 2.7 convolution_bitcast_fusion.1
  268.5 6.1 fusion.36
  274.6 4.4 fusion.34
  280.9 3.6 convert_element_type.40
  286.1 44.5 %reduce-scatter.6.cloned.1.call-done = f32[64,384]{1,0:T(8,128)} async-done(((f32[512,384]{1,0:T(8,128)}), f32[64,384]{1,0:T(8,128)}) %reduce-scatter.6.cloned.1.call-update) | async-done | bytes 98320 | tf_op jit(solution)/shard_map/reduce_scatter | solution.py:191
  332.3 220.5 %all-reduce.19.cloned.1.call-done = (f32[3,1024,512]{2,1,0:T(8,128)}, f32[3,1024,512]{2,1,0:T(8,128)}) async-done(((f32[3,1024,512]{2,1,0:T(8,128)}, f32[3,1024,512]{2,1,0:T(8,128)}), (f32[3,1024,512]{2,1,0:T(8,128)}, f32[3,1024,512]{2,1,0:T(8,128)})) %all-reduce.19.cloned.1.call-update) | async-done | bytes 12582928 | tf_op jit(solution)/shard_map/psum | solution.py:146
  555.2 6.1 multiply_reduce_fusion.2
  562.4 4.0 broadcast_multiply_fusion
  566.4 9.2 %multiply_add_fusion = (f32[3,1024,512]{2,1,0:T(8,128)}, f32[3,1024,512]{2,1,0:T(8,128)}, f32[3,1024,512]{2,1,0:T(8,128)}, f32[3,1024,512]{2,1,0:T(8,128)}) fusion(f32[3,1024,512]{2,1,0:T(8,128)S(1)} %get-tuple-element.100, f32[512]{0:T(512)S(1)} %bitcast.57, f32[512]{0:T(512)S(1)} %bitcast.59, f32[512]{0:T(512)S(1)} %bitcast.55), kind=kLoop, calls=%fused_computation.1 | loop fusion | flops 7864320 | bytes 31463424 | tf_op jit(solution)/shard_map/add | solution.py:28
  578.2 3.6 broadcast_add_fusion
  582.1 6.8 multiply_reduce_fusion.3
  588.8 39.8 %all-reduce.14 = (f32[512]{0:T(512)S(1)}, f32[512]{0:T(512)S(1)}, f32[512]{0:T(512)S(1)}, f32[1536]{0:T(1024)S(1)}, f32[512]{0:T(512)S(1)}, /*index=5*/f32[512]{0:T(512)S(1)}) all-reduce(f32[512]{0:T(512)S(1)} %get-tuple-element.49, f32[512]{0:T(512)S(1)} %get-tuple-element.48, ...), channel_id=3, replica_groups=mesh['dp'=8,'tp'=4] {'dp','tp'}, use_global_device_ids=true, to_apply=%region_15.16.clone | all-reduce | flops 4096 | bytes 32768
  632.3 81.5 %reduce-scatter.10.cloned.1.call-done = f32[16,7]{1,0:T(8,128)} async-done(((f32[512,7]{1,0:T(8,128)}), f32[16,7]{1,0:T(8,128)}) %reduce-scatter.10.cloned.1.call-update) | async-done | bytes 464
  (142 shorter events, 30.9 us)
Async XLA Ops:
  7.2 121.4 %all-gather.4.cloned.1.call-start = ((), (), s32[]{:S(2)}) async-start(), calls=%async_computation.3 | async-start | bytes 3932160 | tf_op jit(solution)/shard_map/all_gather | solution.py:125
  7.9 120.7 %all-gather.6.cloned.1.call-start = ((), (), s32[]{:S(2)}) async-start(), calls=%async_computation.4 | async-start | bytes 3932160 | tf_op jit(solution)/shard_map/all_gather | solution.py:126
  8.7 214.6 %reduce-scatter.8.cloned.1.call-start = ((), (), s32[]{:S(2)}) async-start(), calls=%async_computation.6 | async-start | bytes 884736 | tf_op jit(solution)/shard_map/reduce_scatter | solution.py:192
  157.3 66.0 %copy-start.9 = (f32[64,384]{1,0:T(8,128)S(1)}, f32[64,384]{1,0:T(8,128)}, u32[]{:S(2)}) copy-start(f32[64,384]{1,0:T(8,128)} %param.39) | copy-start | bytes 294916
  157.3 66.0 %copy-start.10 = (f32[64,384]{1,0:T(8,128)S(1)}, f32[64,384]{1,0:T(8,128)}, u32[]{:S(2)}) copy-start(f32[64,384]{1,0:T(8,128)} %param.57) | copy-start | bytes 294916
  157.3 66.0 %copy-start.11 = (f32[64,384]{1,0:T(8,128)S(1)}, f32[64,384]{1,0:T(8,128)}, u32[]{:S(2)}) copy-start(f32[64,384]{1,0:T(8,128)} %param.48) | copy-start | bytes 294916
  160.1 170.5 %reduce-scatter.6.cloned.1.call-start = ((), (), s32[]{:S(2)}) async-start(), calls=%async_computation.5 | async-start | bytes 884736 | tf_op jit(solution)/shard_map/reduce_scatter | solution.py:191
  268.5 284.4 %all-reduce.19.cloned.1.call-start = ((), (), s32[]{:S(2)}) async-start(), calls=%async_computation.8 | async-start | bytes 25165824 | tf_op jit(solution)/shard_map/psum | solution.py:146
  279.1 434.8 %reduce-scatter.10.cloned.1.call-start = ((), (), s32[]{:S(2)}) async-start(), calls=%async_computation.7 | async-start | bytes 270336
  280.9 49.7 %copy-start.8 = (f32[64,384]{1,0:T(8,128)S(1)}, f32[64,384]{1,0:T(8,128)}, u32[]{:S(2)}) copy-start(f32[64,384]{1,0:T(8,128)} %param.37) | copy-start | bytes 294916
  280.9 49.7 %copy-start.12 = (f32[64,384]{1,0:T(8,128)S(1)}, f32[64,384]{1,0:T(8,128)}, u32[]{:S(2)}) copy-start(f32[64,384]{1,0:T(8,128)} %param.55) | copy-start | bytes 294916
  280.9 49.7 %copy-start.13 = (f32[64,384]{1,0:T(8,128)S(1)}, f32[64,384]{1,0:T(8,128)}, u32[]{:S(2)}) copy-start(f32[64,384]{1,0:T(8,128)} %param.46) | copy-start | bytes 294916
  581.9 48.6 %copy-start.27 = (f32[16]{0:T(128)S(1)}, f32[16]{0:T(128)}, u32[]{:S(2)}) copy-start(f32[16]{0:T(128)} %param.40) | copy-start | bytes 196
  581.9 48.6 %copy-start.28 = (f32[16]{0:T(128)S(1)}, f32[16]{0:T(128)}, u32[]{:S(2)}) copy-start(f32[16]{0:T(128)} %param.58) | copy-start | bytes 196
  581.9 48.5 %copy-start.29 = (f32[16]{0:T(128)S(1)}, f32[16]{0:T(128)}, u32[]{:S(2)}) copy-start(f32[16]{0:T(128)} %param.49) | copy-start | bytes 196
  581.9 49.2 %copy-start.30 = (f32[16]{0:T(128)S(1)}, f32[16]{0:T(128)}, u32[]{:S(2)}) copy-start(f32[16]{0:T(128)} %param.41) | copy-start | bytes 196
  582.0 49.1 %copy-start.31 = (f32[16]{0:T(128)S(1)}, f32[16]{0:T(128)}, u32[]{:S(2)}) copy-start(f32[16]{0:T(128)} %param.59) | copy-start | bytes 196
  582.0 49.1 %copy-start.32 = (f32[16]{0:T(128)S(1)}, f32[16]{0:T(128)}, u32[]{:S(2)}) copy-start(f32[16]{0:T(128)} %param.50) | copy-start | bytes 196
  582.0 49.7 %copy-start.33 = (f32[48]{0:T(128)S(1)}, f32[48]{0:T(128)}, u32[]{:S(2)}) copy-start(f32[48]{0:T(128)} %param.38) | copy-start | bytes 580
  582.0 49.7 %copy-start.34 = (f32[48]{0:T(128)S(1)}, f32[48]{0:T(128)}, u32[]{:S(2)}) copy-start(f32[48]{0:T(128)} %param.56) | copy-start | bytes 580
  582.0 49.7 %copy-start.35 = (f32[48]{0:T(128)S(1)}, f32[48]{0:T(128)}, u32[]{:S(2)}) copy-start(f32[48]{0:T(128)} %param.47) | copy-start | bytes 580
  582.0 132.6 %copy-start.14 = (f32[16,7]{0,1:T(8,128)S(1)}, f32[16,7]{0,1:T(8,128)}, u32[]{:S(2)}) copy-start(f32[16,7]{0,1:T(8,128)} %param.33) | copy-start | bytes 1348
  582.0 132.6 %copy-start.16 = (f32[16,7]{0,1:T(8,128)S(1)}, f32[16,7]{0,1:T(8,128)}, u32[]{:S(2)}) copy-start(f32[16,7]{0,1:T(8,128)} %param.51) | copy-start | bytes 1348
  582.0 132.6 %copy-start.17 = (f32[16,7]{0,1:T(8,128)S(1)}, f32[16,7]{0,1:T(8,128)}, u32[]{:S(2)}) copy-start(f32[16,7]{0,1:T(8,128)} %param.42) | copy-start | bytes 1348
  (24 other events, 573.4 us)
Sparse Core Ops, SparseCore 0:
  9.6 31.9 all-gather.3
  43.1 29.1 all-gather.5
  160.2 63.0 reduce-scatter.7
  268.6 62.0 reduce-scatter.5
  333.1 219.6 all-reduce.18
  578.3 135.4 reduce-scatter.9
where the time goes:
time: 723 us; the launch traced here: 722 us
  waiting for transfers between devices  411 us (57%)
  blocking collectives  184 us (25%)
  other arithmetic  73.1 us (10%)
  matrix products  27.2 us (4%)
  between operations  14.6 us (2%)
  local copies, waits for them, and re-layouts  11.8 us (2%)
    psum x1, waiting for transfers between devices, per_device(): branch = lax.psum(partial_out, 'tp') + down_shift  221 us
    unnamed x7, waiting for transfers between devices  83 us
    unnamed x2, blocking collectives  77.1 us
    reduce_scatter x1, waiting for transfers between devices, per_device(): lax.psum_scatter(grad_down, 'dp', scatter_dimension=0, tiled=True)  63 us
    reduce_scatter x1, waiting for transfers between devices, per_device(): lax.psum_scatter(grad_up, 'dp', scatter_dimension=0, tiled=True)  44.5 us
    all_gather x1, blocking collectives, per_device(): lax.all_gather(conv_weight, ('dp', 'tp'), axis=0, tiled=True)  44.2 us
    all_gather x1, blocking collectives, per_device(): lax.all_gather(up_weight.astype(jnp.bfloat16), 'dp', axis=0, tiled=True)  31.3 us
    all_gather x1, blocking collectives, per_device(): lax.all_gather(down_weight.astype(jnp.bfloat16), 'dp', axis=0, tiled=True)  31.1 us
  transfers between devices with their start and end apart: 6, of which 4 were waited for; matrix products, arithmetic and copies ran while one was open for 5% of the time, Pallas kernels for 0%

commit v1 on v0

--- a/solution.py
+++ b/solution.py
@@ -11,6 +11,18 @@
 adam_eps = 1e-08
 weight_decay = 0.1
 update_flags = (False, False, True, False, False, False, False, False, True)
+
+
+def gather_by_bits(x, axis, dim):
+    ways, here, step = (lax.axis_size(axis), lax.axis_index(axis), x.shape[dim])
+    line, have = (x, 1)
+    while have < ways:
+        line = jnp.concatenate(
+            [line, lax.ppermute(line, axis, [(d, (d - have) % ways) for d in range(ways)])],
+            axis=dim,
+        )
+        have = 2 * have
+    return jnp.roll(line, here * step, axis=dim)
 
 
 def conv_apply(padded, tap_weights, conv_shift, frames_out):
@@ -107,7 +119,7 @@
     frame_start = device_rank * quarter_len
     up_rows, down_rows = (
         lax.all_gather(up_weight.astype(jnp.bfloat16), "dp", axis=0, tiled=True),
-        lax.all_gather(down_weight.astype(jnp.bfloat16), "dp", axis=0, tiled=True),
+        gather_by_bits(down_weight.astype(jnp.bfloat16), "dp", 0),
     )
     tap_weights, conv_shift, gain_vector, shift_vector, up_shift, down_shift, scale_vector = (
         lax.all_gather(conv_weight, ("dp", "tp"), axis=0, tiled=True),

time: 723 us -> 699 us (0.967)
  blocking collectives: 184 us -> 147 us
  starting transfers between devices: 0.64 us -> 8.94 us
    all_gather x1 -> x0, blocking collectives: 31.1 us -> none  [per_device(): lax.all_gather(down_weight.astype(jnp.bfloat16), 'dp', axis=0, tiled=True)]
    ppermute x0 -> x3, starting transfers between devices: none -> 8.48 us  [gather_by_bits(): lax.ppermute(line, axis, [(d, (d - have) % ways) for d in range(ways)])]
  transfers between devices with their start and end apart: 6 -> 9, of which waited for: 4 -> 5; matrix products, arithmetic and copies ran while one was open for 5% -> 6% of each run, Pallas kernels for 0% -> 0%
where the time goes in v1:
time: 699 us; the launch traced here: 698 us
  waiting for transfers between devices  418 us (60%)
  blocking collectives  147 us (21%)
  other arithmetic  73 us (10%)
  matrix products  24.1 us (3%)
  between operations  14.7 us (2%)
  local copies, waits for them, and re-layouts  12 us (2%)
  starting transfers between devices  8.94 us (1%)
    psum x1, waiting for transfers between devices, per_device(): branch = lax.psum(partial_out, 'tp') + down_shift  220 us
    unnamed x7, waiting for transfers between devices  83.4 us
    unnamed x2, blocking collectives  77.1 us
    reduce_scatter x1, waiting for transfers between devices, per_device(): lax.psum_scatter(grad_down, 'dp', scatter_dimension=0, tiled=True)  64.4 us
    reduce_scatter x1, waiting for transfers between devices, per_device(): lax.psum_scatter(grad_up, 'dp', scatter_dimension=0, tiled=True)  43.2 us
    all_gather x1, blocking collectives, per_device(): lax.all_gather(conv_weight, ('dp', 'tp'), axis=0, tiled=True)  38.8 us
    all_gather x1, blocking collectives, per_device(): lax.all_gather(up_weight.astype(jnp.bfloat16), 'dp', axis=0, tiled=True)  31.6 us
  transfers between devices with their start and end apart: 9, of which 5 were waited for; matrix products, arithmetic and copies ran while one was open for 6% of the time, Pallas kernels for 0%

profile of v1, /device:TPU:0, one launch (start us, length us, event | category | flops | bytes accessed | tf_op | source)
XLA Modules:
  0.0 698.2 jit_solution(4522713591956412298)
XLA Ops:
  9.7 6.1 collective-permute-start
  15.7 38.8 %all-gather = f32[32,16,7]{1,2,0:T(8,128)S(1)} all-gather(f32[1,16,7]{1,2,0:T(8,128)} %bitcast.60), channel_id=1, replica_groups=mesh['dp'=8,'tp'=4] {'dp','tp'}, dimensions={0}, use_global_device_ids=true | all-gather | bytes 14784 | tf_op jit(solution)/shard_map/all_gather | solution.py:125
  61.4 37.4 %all-reduce.15 = (f32[512]{0:T(512)S(1)}, f32[512]{0:T(512)S(1)}, f32[512]{0:T(512)S(1)}, f32[1536]{0:T(1024)S(1)}, f32[512]{0:T(512)S(1)}, /*index=5*/f32[512]{0:T(512)S(1)}) all-reduce(f32[512]{0:T(512)S(1)} %dynamic-update-slice.1, f32[512]{0:T(512)S(1)} %dynamic-update-slice.3, ...), channel_id=1, replica_groups=mesh['dp'=8,'tp'=4] {'dp','tp'}, use_global_device_ids=true, to_apply=%add.3 | all-reduce | flops 4096 | bytes 32768
  101.1 31.6 %all_gather.36 = bf16[512,384]{1,0:T(8,128)(2,1)S(1)} all-gather(bf16[64,384]{1,0:T(8,128)(2,1)S(1)} %convert_element_type.43), channel_id=1, replica_groups=mesh['dp'=8,'tp'=4] {'dp'}, dimensions={0}, use_global_device_ids=true | all-gather | bytes 442368 | tf_op jit(solution)/shard_map/all_gather | solution.py:121
  132.9 6.5 collective-permute-done.2
  139.6 5.4 convert_multiply_fusion
  145.0 6.0 fusion.63
  153.7 3.1 fusion.31
  156.9 10.9 %multiply_convert_fusion.1 = (bf16[3,1024,384]{2,1,0:T(8,128)(2,1)S(1)}, f32[3,1024,384]{2,1,0:T(8,128)S(1)}) fusion(f32[3,1024,384]{2,1,0:T(8,128)S(1)} %get-tuple-element.124, f32[384]{0:T(512)S(1)} %dynamic_slice.34, u8[1024,384]{1,0:T(8,128)(4,1)S(1)} %get-tuple-element.51, u8[1024,384]{1,0:T(8,128)(4,1)S(1)} %get-tuple-element.50), kind=kLoop, calls=%fused_computation.35 | loop fusion | flops 83755008 | bytes 12584448 | tf_op jit(solution)/shard_map/convert_element_type | solution.py:154
  167.8 3.5 convert_reduce_fusion
  175.7 4.6 convolution_bitcast_fusion
  180.5 5.6 fusion.34
  186.0 4.5 fusion.36
  192.4 3.5 convert_element_type.40
  195.9 43.2 %reduce-scatter.6.cloned.1.call-done = f32[64,384]{1,0:T(8,128)} async-done(((f32[512,384]{1,0:T(8,128)}), f32[64,384]{1,0:T(8,128)}) %reduce-scatter.6.cloned.1.call-update) | async-done | bytes 98320 | tf_op jit(solution)/shard_map/reduce_scatter | solution.py:203
  240.8 64.4 %reduce-scatter.8.cloned.1.call-done = f32[64,384]{1,0:T(8,128)} async-done(((f32[512,384]{1,0:T(8,128)}), f32[64,384]{1,0:T(8,128)}) %reduce-scatter.8.cloned.1.call-update) | async-done | bytes 98320 | tf_op jit(solution)/shard_map/reduce_scatter | solution.py:204
  306.9 220.4 %all-reduce.19.cloned.1.call-done = (f32[3,1024,512]{2,1,0:T(8,128)}, f32[3,1024,512]{2,1,0:T(8,128)}) async-done(((f32[3,1024,512]{2,1,0:T(8,128)}, f32[3,1024,512]{2,1,0:T(8,128)}), (f32[3,1024,512]{2,1,0:T(8,128)}, f32[3,1024,512]{2,1,0:T(8,128)})) %all-reduce.19.cloned.1.call-update) | async-done | bytes 12582928 | tf_op jit(solution)/shard_map/psum | solution.py:158
  529.7 6.1 multiply_reduce_fusion.2
  536.9 3.9 broadcast_multiply_fusion
  540.8 9.2 %multiply_add_fusion = (f32[3,1024,512]{2,1,0:T(8,128)}, f32[3,1024,512]{2,1,0:T(8,128)}, f32[3,1024,512]{2,1,0:T(8,128)}, f32[3,1024,512]{2,1,0:T(8,128)}) fusion(f32[3,1024,512]{2,1,0:T(8,128)S(1)} %get-tuple-element.100, f32[512]{0:T(512)S(1)} %bitcast.55, f32[512]{0:T(512)S(1)} %bitcast.57, f32[512]{0:T(512)S(1)} %bitcast.53), kind=kLoop, calls=%fused_computation.1 | loop fusion | flops 7864320 | bytes 31463424 | tf_op jit(solution)/shard_map/add | solution.py:40
  553.9 3.6 broadcast_add_fusion
  557.7 6.8 multiply_reduce_fusion.3
  564.5 39.7 %all-reduce.14 = (f32[512]{0:T(512)S(1)}, f32[512]{0:T(512)S(1)}, f32[512]{0:T(512)S(1)}, f32[1536]{0:T(1024)S(1)}, f32[512]{0:T(512)S(1)}, /*index=5*/f32[512]{0:T(512)S(1)}) all-reduce(f32[512]{0:T(512)S(1)} %get-tuple-element.49, f32[512]{0:T(512)S(1)} %get-tuple-element.48, ...), channel_id=3, replica_groups=mesh['dp'=8,'tp'=4] {'dp','tp'}, use_global_device_ids=true, to_apply=%region_15.16.clone | all-reduce | flops 4096 | bytes 32768
  608.0 81.9 %reduce-scatter.10.cloned.1.call-done = f32[16,7]{1,0:T(8,128)} async-done(((f32[512,7]{1,0:T(8,128)}), f32[16,7]{1,0:T(8,128)}) %reduce-scatter.10.cloned.1.call-update) | async-done | bytes 464
  (150 shorter events, 36.9 us)
Async XLA Ops:
  7.2 132.4 %all-gather.4.cloned.1.call-start = ((), (), s32[]{:S(2)}) async-start(), calls=%async_computation.3 | async-start | bytes 3932160 | tf_op jit(solution)/shard_map/all_gather | solution.py:137
  7.9 131.6 %all-gather.6.cloned.1.call-start = ((), (), s32[]{:S(2)}) async-start(), calls=%async_computation.4 | async-start | bytes 3932160 | tf_op jit(solution)/shard_map/all_gather | solution.py:138
  8.7 230.4 %reduce-scatter.6.cloned.1.call-start = ((), (), s32[]{:S(2)}) async-start(), calls=%async_computation.5 | async-start | bytes 884736 | tf_op jit(solution)/shard_map/reduce_scatter | solution.py:203
  9.7 89.1 %collective-permute-start = (bf16[64,384]{1,0:T(8,128)(2,1)S(1)}, bf16[64,384]{1,0:T(8,128)(2,1)S(1)}, u32[]{:S(2)}, u32[]{:S(2)}) collective-permute-start(bf16[64,384]{1,0:T(8,128)(2,1)S(1)} %get-tuple-element.102), channel_id=1, source_target_pairs={{0,28},{4,0},{8,4},{12,8},{16,12},{20,16},{24,20},{28,24},{1,29},{... | collective-permute-start | bytes 147464 | tf_op jit(solution)/shard_map/ppermute | solution.py:21
  98.8 33.9 %collective-permute-start.1 = (bf16[128,384]{1,0:T(8,128)(2,1)S(1)}, bf16[128,384]{1,0:T(8,128)(2,1)S(1)}, u32[]{:S(2)}, u32[]{:S(2)}) collective-permute-start(bf16[128,384]{1,0:T(8,128)(2,1)S(1)} %pad_maximum_fusion.1), channel_id=1, source_target_pairs={{0,24},{4,28},{8,0},{12,4},{16,8},{20,12},{24,16},{28,20},{1,25},{... | collective-permute-start | bytes 294920 | tf_op jit(solution)/shard_map/ppermute | solution.py:21
  132.8 6.6 collective-permute-start.2
  175.4 129.7 %reduce-scatter.8.cloned.1.call-start = ((), (), s32[]{:S(2)}) async-start(), calls=%async_computation.6 | async-start | bytes 884736 | tf_op jit(solution)/shard_map/reduce_scatter | solution.py:204
  180.4 346.9 %all-reduce.19.cloned.1.call-start = ((), (), s32[]{:S(2)}) async-start(), calls=%async_computation.8 | async-start | bytes 25165824 | tf_op jit(solution)/shard_map/psum | solution.py:158
  190.5 499.4 %reduce-scatter.10.cloned.1.call-start = ((), (), s32[]{:S(2)}) async-start(), calls=%async_computation.7 | async-start | bytes 270336
  192.4 112.8 %copy-start.9 = (f32[64,384]{1,0:T(8,128)S(1)}, f32[64,384]{1,0:T(8,128)}, u32[]{:S(2)}) copy-start(f32[64,384]{1,0:T(8,128)} %param.39) | copy-start | bytes 294916
  557.5 48.0 %copy-start.23 = (f32[16]{0:T(128)S(1)}, f32[16]{0:T(128)}, u32[]{:S(2)}) copy-start(f32[16]{0:T(128)} %param.36) | copy-start | bytes 196
  557.5 48.0 %copy-start.24 = (f32[16]{0:T(128)S(1)}, f32[16]{0:T(128)}, u32[]{:S(2)}) copy-start(f32[16]{0:T(128)} %param.54) | copy-start | bytes 196
  557.5 48.6 %copy-start.26 = (f32[16]{0:T(128)S(1)}, f32[16]{0:T(128)}, u32[]{:S(2)}) copy-start(f32[16]{0:T(128)} %param.40) | copy-start | bytes 196
  557.6 48.5 %copy-start.27 = (f32[16]{0:T(128)S(1)}, f32[16]{0:T(128)}, u32[]{:S(2)}) copy-start(f32[16]{0:T(128)} %param.58) | copy-start | bytes 196
  557.6 48.5 %copy-start.28 = (f32[16]{0:T(128)S(1)}, f32[16]{0:T(128)}, u32[]{:S(2)}) copy-start(f32[16]{0:T(128)} %param.49) | copy-start | bytes 196
  557.6 49.1 %copy-start.29 = (f32[16]{0:T(128)S(1)}, f32[16]{0:T(128)}, u32[]{:S(2)}) copy-start(f32[16]{0:T(128)} %param.41) | copy-start | bytes 196
  557.6 49.1 %copy-start.30 = (f32[16]{0:T(128)S(1)}, f32[16]{0:T(128)}, u32[]{:S(2)}) copy-start(f32[16]{0:T(128)} %param.59) | copy-start | bytes 196
  557.6 49.1 %copy-start.31 = (f32[16]{0:T(128)S(1)}, f32[16]{0:T(128)}, u32[]{:S(2)}) copy-start(f32[16]{0:T(128)} %param.50) | copy-start | bytes 196
  557.6 49.7 %copy-start.32 = (f32[48]{0:T(128)S(1)}, f32[48]{0:T(128)}, u32[]{:S(2)}) copy-start(f32[48]{0:T(128)} %param.38) | copy-start | bytes 580
  557.6 49.7 %copy-start.33 = (f32[48]{0:T(128)S(1)}, f32[48]{0:T(128)}, u32[]{:S(2)}) copy-start(f32[48]{0:T(128)} %param.56) | copy-start | bytes 580
  557.6 49.7 %copy-start.34 = (f32[48]{0:T(128)S(1)}, f32[48]{0:T(128)}, u32[]{:S(2)}) copy-start(f32[48]{0:T(128)} %param.47) | copy-start | bytes 580
  557.7 133.0 %copy-start.13 = (f32[16,7]{0,1:T(8,128)S(1)}, f32[16,7]{0,1:T(8,128)}, u32[]{:S(2)}) copy-start(f32[16,7]{0,1:T(8,128)} %param.33) | copy-start | bytes 1348
  557.7 133.0 %copy-start.15 = (f32[16,7]{0,1:T(8,128)S(1)}, f32[16,7]{0,1:T(8,128)}, u32[]{:S(2)}) copy-start(f32[16,7]{0,1:T(8,128)} %param.51) | copy-start | bytes 1348
  557.7 133.0 %copy-start.16 = (f32[16,7]{0,1:T(8,128)S(1)}, f32[16,7]{0,1:T(8,128)}, u32[]{:S(2)}) copy-start(f32[16,7]{0,1:T(8,128)} %param.42) | copy-start | bytes 1348
  (24 other events, 542.9 us)
Sparse Core Ops, SparseCore 0:
  9.6 31.9 all-gather.3
  43.1 29.0 all-gather.5
  175.6 63.5 reduce-scatter.5
  242.8 62.2 reduce-scatter.7
  307.6 219.6 all-reduce.18
  554.0 135.8 reduce-scatter.9
